TPU v7x, 32 devices: a whole 2x2x4 slice. The times are simulated.
32 devices in a mesh: wide: 16 (over z, y, core), narrow: 2 (over x).
Axes of the slice: x: 2, y: 2, z: 4, core: 2. Of those that a mesh axis runs over, the one named last changes fastest.
Arguments:
- inputs: bfloat16 [2, 32, 128, 1024], P(None, ('wide', 'narrow')), may hold values from -6 to 6
- out_grad: bfloat16 [2, 32, 128, 1024], P(None, ('wide', 'narrow')), may hold values from -6 to 6
- group_id: int32 [2, 32], P(None, ('wide', 'narrow')), may hold values from 0 to 15
- group_count: int32 [16], replicated, may hold values from 1 to 4
- norm_gain: bfloat16 [4, 1024], P(None, 'narrow'), may hold values from 0.5 to 1.5
- norm_bias: bfloat16 [4, 1024], P(None, 'narrow'), may hold values from -1.25 to 1.25
- w_qkv: bfloat16 [1024, 3072], P('narrow'), may hold values from -0.1875 to 0.1875
- w_out: bfloat16 [1024, 1024], P('narrow'), may hold values from -1.5 to 1.5
- w_up: bfloat16 [1024, 4096], P('narrow'), may hold values from -0.1875 to 0.1875
- w_down: bfloat16 [4096, 1024], P('narrow'), may hold values from -0.09375 to 0.09375
- bias_model: bfloat16 [4, 1024], P(None, 'narrow'), may hold values from -0.625 to 0.625
- bias_up: bfloat16 [4096], P('narrow'), may hold values from -0.625 to 0.625
Outputs:
- output: bfloat16 [2, 32, 128, 1024], P(None, ('wide', 'narrow'))
- grad_input: bfloat16 [2, 32, 128, 1024], P(None, ('wide', 'narrow'))
- grad_norm_gain: float32 [4, 1024], P(None, 'narrow')
- grad_norm_bias: float32 [4, 1024], P(None, 'narrow')
- grad_qkv: float32 [1024, 3072], P('narrow')
- grad_out: float32 [1024, 1024], P('narrow')
- grad_up: float32 [1024, 4096], P('narrow')
- grad_down: float32 [4096, 1024], P('narrow')
- grad_bias_model: float32 [4, 1024], P(None, 'narrow')
- grad_bias_up: float32 [4096], P('narrow')
All inputs are finite; a program needn't handle non-finite values.
Results may differ from a plain program's by a relative error of at most 0.02.
Values may be sent and summed in bfloat16 or wider, within the bound.
No kernel may reach another device: no remote copies, remote signals or barrier semaphores. Data moves between devices by JAX's collectives and lax.ppermute only.
A program may use at most 256 MiB of HBM per device.

v0:
```python
import math
import jax
import jax.numpy as jnp
from jax import lax
from jax.sharding import PartitionSpec as P

HEADS = 16
EPSILON = 1e-05
RELAX = 32.0


def layer_norm(value, gain, shift):
    average = jnp.mean(value, axis=-1, keepdims=True)
    centred = value - average
    spread = jnp.mean(centred * centred, axis=-1, keepdims=True)
    return centred * lax.rsqrt(spread + EPSILON) * gain + shift


def exact_gelu(value):
    return jax.nn.gelu(value, approximate=False)


def forward_product(left, right):
    return jnp.dot(left, right, preferred_element_type=jnp.float32)


def back_product(grad, weight):
    return lax.dot_general(
        grad, weight, (((1,), (1,)), ((), ())), preferred_element_type=jnp.float32
    )


def weight_grad(left, grad):
    return lax.dot_general(left, grad, (((0,), (0,)), ((), ())), preferred_element_type=jnp.float32)


def column_sum(grad):
    return jnp.sum(grad.astype(jnp.float32), axis=0)


def split_heads(qkv, seqs, heads):
    length = qkv.shape[0] // seqs
    width = qkv.shape[1] // 3
    parts = qkv.reshape(seqs, length, 3, heads, width // heads)
    return (parts[:, :, 0], parts[:, :, 1], parts[:, :, 2])


def raw_scores(query, keys):
    length = query.shape[1]
    scale = RELAX * math.sqrt(query.shape[-1])
    scores = jnp.einsum("sqhd,skhd->shqk", query, keys, preferred_element_type=jnp.float32) / scale
    rows = lax.broadcasted_iota(jnp.int32, (length, length), 0)
    columns = lax.broadcasted_iota(jnp.int32, (length, length), 1)
    return jnp.where(columns <= rows, scores, -1000000000.0)


def forward_pass(block, full, seqs, heads):
    gain = full[0].astype(jnp.float32)
    shift = full[1].astype(jnp.float32)
    bias = full[6].astype(jnp.float32)
    bias_hidden = full[7].astype(jnp.float32)
    tokens, width = block.shape
    qkv_bias = jnp.concatenate([bias[0], jnp.zeros((width,), jnp.float32), bias[1]])
    block_value = block.astype(jnp.float32)
    first = layer_norm(block_value, gain[0], shift[0]).astype(jnp.bfloat16)
    qkv = (forward_product(first, full[2]) + qkv_bias).astype(jnp.bfloat16)
    query, keys, values = split_heads(qkv, seqs, heads)
    scores = raw_scores(query, keys)
    top = jnp.max(scores, axis=-1, keepdims=True)
    exps = jnp.exp(RELAX * (scores - top))
    total = jnp.sum(exps, axis=-1, keepdims=True)
    logsum = jnp.log(total)
    weights = (exps / total).astype(jnp.bfloat16)
    mixed = jnp.einsum("shqk,skhd->sqhd", weights, values, preferred_element_type=jnp.float32)
    mixed = mixed.reshape(tokens, width).astype(jnp.bfloat16)
    branch = forward_product(mixed, full[3]) + bias[2]
    middle = block_value + layer_norm(branch, gain[1], shift[1])
    third = layer_norm(middle, gain[2], shift[2]).astype(jnp.bfloat16)
    hidden = forward_product(third, full[4]) + bias_hidden
    active = exact_gelu(hidden).astype(jnp.bfloat16)
    second = forward_product(active, full[5]) + bias[3]
    result = middle + layer_norm(second, gain[3], shift[3])
    kept = (
        block_value,
        first,
        qkv,
        top,
        logsum,
        mixed,
        branch,
        middle,
        third,
        hidden,
        active,
        second,
    )
    return (result, kept)


def attention_back(qkv, top, logsum, grad_mixed, seqs, heads):
    query, keys, values = split_heads(qkv, seqs, heads)
    scores = raw_scores(query, keys)
    probs = jnp.exp(RELAX * (scores - top) - logsum)
    weights = probs.astype(jnp.bfloat16)
    tokens, width = grad_mixed.shape
    grad_heads = grad_mixed.reshape(seqs, tokens // seqs, heads, width // heads)
    grad_weights = jnp.einsum(
        "sqhd,skhd->shqk", grad_heads, values, preferred_element_type=jnp.float32
    )
    inner = jnp.sum(probs * grad_weights, axis=-1, keepdims=True)
    grad_scores = (RELAX * probs * (grad_weights - inner)).astype(jnp.bfloat16)
    scale = RELAX * math.sqrt(query.shape[-1])
    grad_query = (
        jnp.einsum("shqk,skhd->sqhd", grad_scores, keys, preferred_element_type=jnp.float32) / scale
    )
    grad_keys = (
        jnp.einsum("shqk,sqhd->skhd", grad_scores, query, preferred_element_type=jnp.float32)
        / scale
    )
    grad_values = jnp.einsum(
        "shqk,sqhd->skhd", weights, grad_heads, preferred_element_type=jnp.float32
    )
    stacked = jnp.stack([grad_query, grad_keys, grad_values], axis=2)
    return stacked.reshape(tokens, 3 * width).astype(jnp.bfloat16)


def backward_pass(cotangent, full, kept, seqs, heads):
    block_value, first, qkv, top, logsum, mixed, branch, middle, third, hidden, active, second = (
        kept
    )
    gain = full[0].astype(jnp.float32)
    shift = full[1].astype(jnp.float32)
    width = block_value.shape[1]
    unused_last, pull_last = jax.vjp(layer_norm, second, gain[3], shift[3])
    grad_second, gain_last, shift_last = pull_last(cotangent)
    grad_second = grad_second.astype(jnp.bfloat16)
    grad_down = weight_grad(active, grad_second)
    bias_down = column_sum(grad_second)
    grad_active = back_product(grad_second, full[5])
    unused_gelu, pull_gelu = jax.vjp(exact_gelu, hidden)
    grad_hidden = pull_gelu(grad_active)[0].astype(jnp.bfloat16)
    grad_up = weight_grad(third, grad_hidden)
    bias_hidden = column_sum(grad_hidden)
    grad_third = back_product(grad_hidden, full[4])
    unused_third, pull_third = jax.vjp(layer_norm, middle, gain[2], shift[2])
    grad_inner, gain_third, shift_third = pull_third(grad_third)
    grad_middle = cotangent + grad_inner
    unused_branch, pull_branch = jax.vjp(layer_norm, branch, gain[1], shift[1])
    grad_branch, gain_branch, shift_branch = pull_branch(grad_middle)
    grad_branch = grad_branch.astype(jnp.bfloat16)
    grad_out = weight_grad(mixed, grad_branch)
    bias_out = column_sum(grad_branch)
    grad_mixed = back_product(grad_branch, full[3]).astype(jnp.bfloat16)
    grad_qkv = attention_back(qkv, top, logsum, grad_mixed, seqs, heads)
    grad_project = weight_grad(first, grad_qkv)
    qkv_sums = column_sum(grad_qkv)
    grad_first = back_product(grad_qkv, full[2])
    unused_first, pull_first = jax.vjp(layer_norm, block_value, gain[0], shift[0])
    grad_block, gain_first, shift_first = pull_first(grad_first)
    grad_input = grad_middle + grad_block
    grad_gain = jnp.stack([gain_first, gain_branch, gain_third, gain_last])
    grad_shift = jnp.stack([shift_first, shift_branch, shift_third, shift_last])
    grad_bias = jnp.stack([qkv_sums[:width], qkv_sums[2 * width :], bias_out, bias_down])
    return (
        grad_input,
        (grad_gain, grad_shift, grad_project, grad_out, grad_up, grad_down, grad_bias, bias_hidden),
    )


def on_device(
    inputs,
    out_grad,
    group_id,
    group_count,
    norm_gain,
    norm_bias,
    w_qkv,
    w_out,
    w_up,
    w_down,
    bias_model,
    bias_up,
):
    micros, seqs, length, width = inputs.shape
    heads = HEADS
    tokens = seqs * length
    matches = (
        group_id[:, :, None] == jnp.arange(group_count.shape[0], dtype=jnp.int32)[None, None, :]
    )
    counts = jnp.sum(jnp.where(matches, group_count[None, None, :], 0), axis=-1)
    seq_scale = 1.0 / counts.astype(jnp.float32)
    results = []
    grad_inputs = []
    totals = None
    for micro in range(micros):
        full = (
            lax.all_gather(norm_gain, "narrow", axis=1, tiled=True),
            lax.all_gather(norm_bias, "narrow", axis=1, tiled=True),
            lax.all_gather(w_qkv, "narrow", axis=0, tiled=True),
            lax.all_gather(w_out, "narrow", axis=0, tiled=True),
            lax.all_gather(w_up, "narrow", axis=0, tiled=True),
            lax.all_gather(w_down, "narrow", axis=0, tiled=True),
            lax.all_gather(bias_model, "narrow", axis=1, tiled=True),
            lax.all_gather(bias_up, "narrow", axis=0, tiled=True),
        )
        result, kept = forward_pass(inputs[micro].reshape(tokens, width), full, seqs, heads)
        results.append(result.reshape(seqs, length, width).astype(jnp.bfloat16))
        full = (
            lax.all_gather(norm_gain, "narrow", axis=1, tiled=True),
            lax.all_gather(norm_bias, "narrow", axis=1, tiled=True),
            lax.all_gather(w_qkv, "narrow", axis=0, tiled=True),
            lax.all_gather(w_out, "narrow", axis=0, tiled=True),
            lax.all_gather(w_up, "narrow", axis=0, tiled=True),
            lax.all_gather(w_down, "narrow", axis=0, tiled=True),
            lax.all_gather(bias_model, "narrow", axis=1, tiled=True),
            lax.all_gather(bias_up, "narrow", axis=0, tiled=True),
        )
        cotangent = out_grad[micro].astype(jnp.float32) * seq_scale[micro][:, None, None]
        grad_input, grads = backward_pass(cotangent.reshape(tokens, width), full, kept, seqs, heads)
        grad_inputs.append(grad_input.reshape(seqs, length, width).astype(jnp.bfloat16))
        shares = (
            lax.psum_scatter(
                grads[0].astype(jnp.bfloat16), "narrow", scatter_dimension=1, tiled=True
            ).astype(jnp.float32),
            lax.psum_scatter(
                grads[1].astype(jnp.bfloat16), "narrow", scatter_dimension=1, tiled=True
            ).astype(jnp.float32),
            lax.psum_scatter(
                grads[2].astype(jnp.bfloat16), "narrow", scatter_dimension=0, tiled=True
            ).astype(jnp.float32),
            lax.psum_scatter(
                grads[3].astype(jnp.bfloat16), "narrow", scatter_dimension=0, tiled=True
            ).astype(jnp.float32),
            lax.psum_scatter(
                grads[4].astype(jnp.bfloat16), "narrow", scatter_dimension=0, tiled=True
            ).astype(jnp.float32),
            lax.psum_scatter(
                grads[5].astype(jnp.bfloat16), "narrow", scatter_dimension=0, tiled=True
            ).astype(jnp.float32),
            lax.psum_scatter(
                grads[6].astype(jnp.bfloat16), "narrow", scatter_dimension=1, tiled=True
            ).astype(jnp.float32),
            lax.psum_scatter(
                grads[7].astype(jnp.bfloat16), "narrow", scatter_dimension=0, tiled=True
            ).astype(jnp.float32),
        )
        if totals is None:
            totals = tuple(shares)
        else:
            totals = tuple((left + right for left, right in zip(totals, shares)))
    summed = (
        lax.psum(totals[0].astype(jnp.bfloat16), "wide").astype(jnp.float32),
        lax.psum(totals[1].astype(jnp.bfloat16), "wide").astype(jnp.float32),
        lax.psum(totals[2].astype(jnp.bfloat16), "wide").astype(jnp.float32),
        lax.psum(totals[3].astype(jnp.bfloat16), "wide").astype(jnp.float32),
        lax.psum(totals[4].astype(jnp.bfloat16), "wide").astype(jnp.float32),
        lax.psum(totals[5].astype(jnp.bfloat16), "wide").astype(jnp.float32),
        lax.psum(totals[6].astype(jnp.bfloat16), "wide").astype(jnp.float32),
        lax.psum(totals[7].astype(jnp.bfloat16), "wide").astype(jnp.float32),
    )
    output = jnp.stack(results)
    grad_all = jnp.stack(grad_inputs)
    return (
        output,
        grad_all,
        summed[0],
        summed[1],
        summed[2],
        summed[3],
        summed[4],
        summed[5],
        summed[6],
        summed[7],
    )


def solution(mesh):
    return jax.shard_map(
        on_device,
        mesh=mesh,
        in_specs=(
            P(None, ("wide", "narrow"), None, None),
            P(None, ("wide", "narrow"), None, None),
            P(None, ("wide", "narrow")),
            P(),
            P(None, "narrow"),
            P(None, "narrow"),
            P("narrow", None),
            P("narrow", None),
            P("narrow", None),
            P("narrow", None),
            P(None, "narrow"),
            P("narrow"),
        ),
        out_specs=(
            P(None, ("wide", "narrow"), None, None),
            P(None, ("wide", "narrow"), None, None),
            P(None, "narrow"),
            P(None, "narrow"),
            P("narrow", None),
            P("narrow", None),
            P("narrow", None),
            P("narrow", None),
            P(None, "narrow"),
            P("narrow"),
        ),
        check_vma=False,
    )
```

profile of v0, /device:TPU:0, one launch (start us, length us, event | category | flops | bytes accessed | tf_op | source)
XLA Modules:
  0.0 1364.5 jit_solution(11387868374793793821)
XLA Ops:
  10.1 5.3 all_gather.19
  15.4 4.4 all_gather.22
  19.8 4.4 all_gather.17
  24.2 4.6 all_gather.16
  30.1 62.6 %all-gather.5.cloned.1.call-done = bf16[1024,3072]{1,0:T(8,128)(2,1)} async-done(((bf16[512,3072]{1,0:T(8,128)(2,1)}), bf16[1024,3072]{1,0:T(8,128)(2,1)}) %all-gather.5.cloned.1.call-update) | async-done | bytes 6291472 | tf_op jit(solution)/shard_map/all_gather | solution.py:199
  92.7 3.9 fusion.2
  97.0 4.2 fusion.3
  104.4 23.1 %all-gather.7.cloned.1.call-done = bf16[1024,1024]{1,0:T(8,128)(2,1)} async-done(((bf16[512,1024]{1,0:T(8,128)(2,1)}), bf16[1024,1024]{1,0:T(8,128)(2,1)}) %all-gather.7.cloned.1.call-update) | async-done | bytes 2097168 | tf_op jit(solution)/shard_map/all_gather | solution.py:200
  138.8 94.2 %all-gather.9.cloned.1.call-done = bf16[1024,4096]{1,0:T(8,128)(2,1)} async-done(((bf16[512,4096]{1,0:T(8,128)(2,1)}), bf16[1024,4096]{1,0:T(8,128)(2,1)}) %all-gather.9.cloned.1.call-update) | async-done | bytes 8388624 | tf_op jit(solution)/shard_map/all_gather | solution.py:201
  233.0 9.9 multiply_convert_fusion
  242.9 95.5 %all-gather.11.cloned.1.call-done = bf16[4096,1024]{1,0:T(8,128)(2,1)} async-done(((bf16[2048,1024]{1,0:T(8,128)(2,1)}), bf16[4096,1024]{1,0:T(8,128)(2,1)}) %all-gather.11.cloned.1.call-update) | async-done | bytes 8388624 | tf_op jit(solution)/shard_map/all_gather | solution.py:202
  338.4 5.2 fusion.153
  344.5 9.1 multiply_convert_fusion.1
  360.7 5.7 fusion.126
  366.5 2.9 fusion.155
  369.4 5.7 fusion.125
  376.0 3.6 multiply_reduce_fusion.4
  388.1 3.0 convolution_convert_fusion.7
  395.5 2.9 convolution_bitcast_fusion
  402.8 4.7 convolution_convert_fusion.4
  414.4 4.6 convolution_convert_fusion.5
  420.1 7.1 convolution_convert_fusion.2
  427.2 7.2 convolution_convert_fusion.3
  435.7 5.6 convolution_convert_fusion
  442.6 5.6 convolution_convert_fusion.1
  450.7 5.1 fusion.156
  455.7 5.1 fusion.53
  468.0 2.9 add_convert_fusion.3
  470.9 62.1 %reduce-scatter.29.cloned.1.call-done = bf16[512,3072]{1,0:T(8,128)(2,1)} async-done(((bf16[1024,3072]{1,0:T(8,128)(2,1)}), bf16[512,3072]{1,0:T(8,128)(2,1)}) %reduce-scatter.29.cloned.1.call-update) | async-done | bytes 3145744 | tf_op jit(solution)/shard_map/reduce_scatter | solution.py:228
  533.0 79.5 %reduce-scatter.27.cloned.1.call-done = bf16[512,3072]{1,0:T(8,128)(2,1)} async-done(((bf16[1024,3072]{1,0:T(8,128)(2,1)}), bf16[512,3072]{1,0:T(8,128)(2,1)}) %reduce-scatter.27.cloned.1.call-update) | async-done | bytes 3145744 | tf_op jit(solution)/shard_map/reduce_scatter | solution.py:228
  612.5 5.7 add_convert_fusion.2
  618.2 96.6 %reduce-scatter.37.cloned.1.call-done = bf16[512,4096]{1,0:T(8,128)(2,1)} async-done(((bf16[1024,4096]{1,0:T(8,128)(2,1)}), bf16[512,4096]{1,0:T(8,128)(2,1)}) %reduce-scatter.37.cloned.1.call-update) | async-done | bytes 4194320 | tf_op jit(solution)/shard_map/reduce_scatter | solution.py:234
  714.7 102.1 %reduce-scatter.35.cloned.1.call-done = bf16[512,4096]{1,0:T(8,128)(2,1)} async-done(((bf16[1024,4096]{1,0:T(8,128)(2,1)}), bf16[512,4096]{1,0:T(8,128)(2,1)}) %reduce-scatter.35.cloned.1.call-update) | async-done | bytes 4194320 | tf_op jit(solution)/shard_map/reduce_scatter | solution.py:234
  816.8 7.2 add_convert_fusion.1
  824.1 94.4 %reduce-scatter.41.cloned.1.call-done = bf16[2048,1024]{1,0:T(8,128)(2,1)} async-done(((bf16[4096,1024]{1,0:T(8,128)(2,1)}), bf16[2048,1024]{1,0:T(8,128)(2,1)}) %reduce-scatter.41.cloned.1.call-update) | async-done | bytes 4194320 | tf_op jit(solution)/shard_map/reduce_scatter | solution.py:237
  918.5 101.5 %reduce-scatter.39.cloned.1.call-done = bf16[2048,1024]{1,0:T(8,128)(2,1)} async-done(((bf16[4096,1024]{1,0:T(8,128)(2,1)}), bf16[2048,1024]{1,0:T(8,128)(2,1)}) %reduce-scatter.39.cloned.1.call-update) | async-done | bytes 4194320 | tf_op jit(solution)/shard_map/reduce_scatter | solution.py:237
  1020.0 7.6 add_convert_fusion
  1029.5 6.9 all-reduce.4
  1039.5 8.4 reduce-scatter.43.cloned.1.call-done
  1048.9 12.9 reduce-scatter.49.cloned.1.call-done
  1062.8 12.9 reduce-scatter.47.cloned.1.call-done
  1076.7 12.9 reduce-scatter.53.cloned.1.call-done
  1090.5 12.9 reduce-scatter.51.cloned.1.call-done
  1104.5 64.5 %all-reduce.2 = (bf16[4,512]{1,0:T(4,128)(2,1)S(1)}, bf16[4,512]{1,0:T(4,128)(2,1)S(1)}, bf16[4,512]{1,0:T(4,128)(2,1)S(1)}, bf16[2048]{0:T(1024)(128)(2,1)S(1)}) all-reduce(bf16[4,512]{1,0:T(4,128)(2,1)S(1)} %add_convert_fusion.19, bf16[4,512]{1,0:T(4,128)(2,1)S(1)} %add_convert_fusion.18, ...), channel_id=1, replica_groups=mesh['wide'=16,'narrow'=2] {'wide'}, use_global_device_ids=true, to_apply=%region_49.50 | all-reduce | flops 8192 | bytes 32768 | tf_op jit(solution)/shard_map/psum | solution.py:252
  1171.4 170.0 %all-reduce.7.cloned.1.call-done = (bf16[512,3072]{1,0:T(8,128)(2,1)}, bf16[512,1024]{1,0:T(8,128)(2,1)}, bf16[512,4096]{1,0:T(8,128)(2,1)}, bf16[2048,1024]{1,0:T(8,128)(2,1)}) async-done(((bf16[512,3072]{1,0:T(8,128)(2,1)}, bf16[512,1024]{1,0:T(8,128)(2,1)}, bf16[512,4096]{1,0:T(8,128)(2,1)}, bf16[2048,1024]{1,0:T(8,128)(2,1)}), (bf16[512,3072]{1,0:T(8,128)(2,1)}, bf16[512,1024]{1,0:T(8,128)(2,1)}, ...) | async-done | bytes 12582928 | tf_op jit(solution)/shard_map/psum | solution.py:254
  1341.4 5.5 convert_element_type.454
  1348.6 4.5 convert_element_type.466
  1353.0 4.4 convert_element_type.472
  (319 shorter events, 77.8 us)
Async XLA Ops:
  7.2 85.5 %all-gather.5.cloned.1.call-start = ((), (), s32[]{:S(2)}) async-start(), calls=%async_computation.14 | async-start | bytes 9437184 | tf_op jit(solution)/shard_map/all_gather | solution.py:199
  7.9 119.5 %all-gather.7.cloned.1.call-start = ((), (), s32[]{:S(2)}) async-start(), calls=%async_computation.15 | async-start | bytes 3145728 | tf_op jit(solution)/shard_map/all_gather | solution.py:200
  8.7 224.3 %all-gather.9.cloned.1.call-start = ((), (), s32[]{:S(2)}) async-start(), calls=%async_computation.16 | async-start | bytes 12582912 | tf_op jit(solution)/shard_map/all_gather | solution.py:201
  9.4 6.0 copy-start.47
  9.4 10.4 copy-start.48
  9.4 14.7 %copy-start.49 = (bf16[4,512]{1,0:T(4,128)(2,1)S(1)}, bf16[4,512]{1,0:T(4,128)(2,1)}, u32[]{:S(2)}) copy-start(bf16[4,512]{1,0:T(4,128)(2,1)} %param.16) | copy-start | bytes 12292
  9.4 19.3 %copy-start.2 = (bf16[2,1,128,1024]{3,2,1,0:T(8,128)(2,1)S(1)}, bf16[2,1,128,1024]{3,2,1,0:T(8,128)(2,1)}, u32[]{:S(2)}) copy-start(bf16[2,1,128,1024]{3,2,1,0:T(8,128)(2,1)} %param.12) | copy-start | bytes 1572868
  9.4 19.4 %copy-start.60 = (s32[16]{0:T(128)S(1)}, s32[16]{0:T(128)}, u32[]{:S(2)}) copy-start(s32[16]{0:T(128)} %param.15) | copy-start | bytes 196
  9.5 19.4 %copy-start.61 = (s32[2,1]{0,1:T(1,128)S(1)}, s32[2,1]{0,1:T(1,128)}, u32[]{:S(2)}) copy-start(s32[2,1]{0,1:T(1,128)} %param.14) | copy-start | bytes 28
  9.5 328.9 %all-gather.11.cloned.1.call-start = ((), (), s32[]{:S(2)}) async-start(), calls=%async_computation.17 | async-start | bytes 12582912 | tf_op jit(solution)/shard_map/all_gather | solution.py:202
  10.0 457.9 %reduce-scatter.33.cloned.1.call-start = ((), (), s32[]{:S(2)}) async-start(), calls=%async_computation.21 | async-start | bytes 3145728 | tf_op jit(solution)/shard_map/reduce_scatter | solution.py:231
  29.4 67.2 %copy-start.52 = (f32[128]{0:T(128)}, f32[128]{0:T(128)S(1)}, u32[]{:S(2)}) copy-start(f32[128]{0:T(128)S(1)} %get-tuple-element.41) | copy-start | bytes 1540
  96.9 6.4 copy-start.18
  101.5 30.6 %copy-start.20 = (bf16[128,3072]{0,1:T(8,128)(2,1)}, bf16[128,3072]{0,1:T(8,128)(2,1)S(1)}, u32[]{:S(2)}) copy-start(bf16[128,3072]{0,1:T(8,128)(2,1)S(1)} %copy.66) | copy-start | bytes 2359300
  104.4 27.7 %copy-start.34 = (bf16[16,64,128]{2,1,0:T(8,128)(2,1)}, bf16[16,64,128]{2,1,0:T(8,128)(2,1)S(1)}, u32[]{:S(2)}) copy-start(bf16[16,64,128]{2,1,0:T(8,128)(2,1)S(1)} %convolution_convert_fusion.11) | copy-start | bytes 786436
  130.6 6.5 copy-start.54
  137.0 105.9 %copy-start.56 = (f32[128]{0:T(128)}, f32[128]{0:T(128)S(1)}, u32[]{:S(2)}) copy-start(f32[128]{0:T(128)S(1)} %multiply_reduce_fusion.14) | copy-start | bytes 1540
  138.8 104.2 %copy-start.58 = (f32[128]{0:T(128)}, f32[128]{0:T(128)S(1)}, u32[]{:S(2)}) copy-start(f32[128]{0:T(128)S(1)} %multiply_reduce_fusion.16) | copy-start | bytes 1540
  338.4 6.1 copy-start.1
  338.4 16.2 %slice-start = ((s8[8388608]{0:T(1024)(128)(4,1)}), s8[4194304]{0:T(1024)(128)(4,1)S(1)}, s32[]{:S(2)}) async-start(s8[8388608]{0:T(1024)(128)(4,1)} %bitcast.286), calls=%async_computation.33 | async-start | bytes 8388608
  344.5 10.1 slice-start.1
  360.6 5.9 copy-start.40
  360.7 8.7 copy-start.38
  376.0 3.8 copy-start.59
  386.9 81.1 %reduce-scatter.31.cloned.1.call-start = ((), (), s32[]{:S(2)}) async-start(), calls=%async_computation.20 | async-start | bytes 3145728 | tf_op jit(solution)/shard_map/reduce_scatter | solution.py:231
  391.1 141.9 %reduce-scatter.29.cloned.1.call-start = ((), (), s32[]{:S(2)}) async-start(), calls=%async_computation.19 | async-start | bytes 9437184 | tf_op jit(solution)/shard_map/reduce_scatter | solution.py:228
  407.5 205.0 %reduce-scatter.27.cloned.1.call-start = ((), (), s32[]{:S(2)}) async-start(), calls=%async_computation.18 | async-start | bytes 9437184 | tf_op jit(solution)/shard_map/reduce_scatter | solution.py:228
  419.1 295.7 %reduce-scatter.37.cloned.1.call-start = ((), (), s32[]{:S(2)}) async-start(), calls=%async_computation.23 | async-start | bytes 12582912 | tf_op jit(solution)/shard_map/reduce_scatter | solution.py:234
  427.2 389.6 %reduce-scatter.35.cloned.1.call-start = ((), (), s32[]{:S(2)}) async-start(), calls=%async_computation.22 | async-start | bytes 12582912 | tf_op jit(solution)/shard_map/reduce_scatter | solution.py:234
  434.5 484.0 %reduce-scatter.41.cloned.1.call-start = ((), (), s32[]{:S(2)}) async-start(), calls=%async_computation.25 | async-start | bytes 12582912 | tf_op jit(solution)/shard_map/reduce_scatter | solution.py:237
  441.3 578.7 %reduce-scatter.39.cloned.1.call-start = ((), (), s32[]{:S(2)}) async-start(), calls=%async_computation.24 | async-start | bytes 12582912 | tf_op jit(solution)/shard_map/reduce_scatter | solution.py:237
  448.2 590.3 %reduce-scatter.45.cloned.1.call-start = ((), (), s32[]{:S(2)}) async-start(), calls=%async_computation.27 | async-start | bytes 393216
  455.7 5.1 copy-start.53
  455.7 5.2 copy-start.51
  455.7 6.7 copy-start.45
  462.5 585.4 %reduce-scatter.43.cloned.1.call-start = ((), (), s32[]{:S(2)}) async-start(), calls=%async_computation.26 | async-start | bytes 393216
  463.5 598.3 %reduce-scatter.49.cloned.1.call-start = ((), (), s32[]{:S(2)}) async-start(), calls=%async_computation.29 | async-start | bytes 393216
  464.5 611.1 %reduce-scatter.47.cloned.1.call-start = ((), (), s32[]{:S(2)}) async-start(), calls=%async_computation.28 | async-start | bytes 393216
  465.7 623.8 %reduce-scatter.53.cloned.1.call-start = ((), (), s32[]{:S(2)}) async-start(), calls=%async_computation.31 | async-start | bytes 393216
  466.9 636.5 %reduce-scatter.51.cloned.1.call-start = ((), (), s32[]{:S(2)}) async-start(), calls=%async_computation.30 | async-start | bytes 393216
  467.9 873.5 %all-reduce.7.cloned.1.call-start = ((), (), s32[]{:S(2)}) async-start(), calls=%async_computation.32 | async-start | bytes 25165824 | tf_op jit(solution)/shard_map/psum | solution.py:254
  1027.6 8.8 copy-start.36
  1027.6 8.8 copy-start.37
  1027.6 9.7 copy-start.23
  1027.6 9.7 copy-start.25
  1341.4 5.5 copy-start.33
  1341.4 7.1 copy-start.27
  1348.5 4.5 copy-start.26
  (36 other events, 58.3 us)
Sparse Core Ops, SparseCore 0:
  9.5 83.1 all-gather.4
  94.2 33.1 all-gather.6
  129.0 103.9 all-gather.8
  234.4 103.9 all-gather.10
  387.0 31.8 reduce-scatter.32
  421.0 31.8 reduce-scatter.30
  455.8 77.1 reduce-scatter.28
  535.3 77.1 reduce-scatter.26
  615.4 99.3 reduce-scatter.36
  717.4 99.3 reduce-scatter.34
  819.1 99.3 reduce-scatter.40
  920.6 99.3 reduce-scatter.38
  1022.2 11.7 reduce-scatter.44
  1036.1 11.7 reduce-scatter.42
  1050.0 11.7 reduce-scatter.48
  1063.9 11.7 reduce-scatter.46
  1077.7 11.7 reduce-scatter.52
  1091.6 11.7 reduce-scatter.50
  1108.6 232.8 all-reduce.6
where the time goes:
time: 1370 us; the launch traced here: 1360 us
  waiting for transfers between devices  1040 us (76%)
  matrix products  125 us (9%)
  blocking collectives  90 us (7%)
  other arithmetic  59 us (4%)
  local copies, waits for them, and re-layouts  28.8 us (2%)
  between operations  16.4 us (1%)
    reduce_scatter x2, waiting for transfers between devices, on_device(): lax.psum_scatter(grads[4].astype(jnp.bfloat16), 'narrow', scatter_dimensi...  199 us
    reduce_scatter x2, waiting for transfers between devices, on_device(): lax.psum_scatter(grads[5].astype(jnp.bfloat16), 'narrow', scatter_dimensi...  196 us
    psum x1, waiting for transfers between devices, on_device(): lax.psum(totals[2].astype(jnp.bfloat16), 'wide').astype(jnp.float32)  170 us
    reduce_scatter x2, waiting for transfers between devices, on_device(): lax.psum_scatter(grads[2].astype(jnp.bfloat16), 'narrow', scatter_dimensi...  142 us
    all_gather x1, waiting for transfers between devices, on_device(): lax.all_gather(w_down, 'narrow', axis=0, tiled=True)  95.5 us
    all_gather x1, waiting for transfers between devices, on_device(): lax.all_gather(w_up, 'narrow', axis=0, tiled=True)  94.2 us
    psum x1, blocking collectives, on_device(): lax.psum(totals[0].astype(jnp.bfloat16), 'wide').astype(jnp.float32)  64.5 us
    unnamed x25, waiting for transfers between devices  62.7 us
  transfers between devices with their start and end apart: 19, of which 16 were waited for; matrix products, arithmetic and copies ran while one was open for 10% of the time, Pallas kernels for 0%

commit v1 on v0

--- a/solution.py
+++ b/solution.py
@@ -248,8 +248,9 @@
             totals = tuple(shares)
         else:
             totals = tuple((left + right for left, right in zip(totals, shares)))
+    see_row = lambda unit, chip_axis: jnp.sum(jax.lax.all_gather(unit, axis_name=chip_axis), axis=0)
     summed = (
-        lax.psum(totals[0].astype(jnp.bfloat16), "wide").astype(jnp.float32),
+        see_row(totals[0].astype(jnp.bfloat16), "wide").astype(jnp.float32),
         lax.psum(totals[1].astype(jnp.bfloat16), "wide").astype(jnp.float32),
         lax.psum(totals[2].astype(jnp.bfloat16), "wide").astype(jnp.float32),
         lax.psum(totals[3].astype(jnp.bfloat16), "wide").astype(jnp.float32),

time: 1370 us -> 1370 us (level)
  blocking collectives: 90 us -> 111 us
  waiting for transfers between devices: 1040 us -> 1020 us
    unnamed x25, waiting for transfers between devices: 62.7 us -> 40.6 us
    all_gather x0 -> x1, blocking collectives: none -> 21.5 us  [on_device(): jax.lax.all_gather(unit, axis_name=chip_axis)]
  transfers between devices with their start and end apart: 19 -> 19, of which waited for: 16 -> 15; matrix products, arithmetic and copies ran while one was open for 10% -> 10% of each run, Pallas kernels for 0% -> 0%
where the time goes in v1:
time: 1370 us; the launch traced here: 1360 us
  waiting for transfers between devices  1020 us (74%)
  matrix products  125 us (9%)
  blocking collectives  111 us (8%)
  other arithmetic  59.1 us (4%)
  local copies, waits for them, and re-layouts  28.7 us (2%)
  between operations  16.1 us (1%)
    reduce_scatter x2, waiting for transfers between devices, on_device(): lax.psum_scatter(grads[4].astype(jnp.bfloat16), 'narrow', scatter_dimensi...  199 us
    reduce_scatter x2, waiting for transfers between devices, on_device(): lax.psum_scatter(grads[5].astype(jnp.bfloat16), 'narrow', scatter_dimensi...  196 us
    psum x1, waiting for transfers between devices, on_device(): lax.psum(totals[2].astype(jnp.bfloat16), 'wide').astype(jnp.float32)  171 us
    reduce_scatter x2, waiting for transfers between devices, on_device(): lax.psum_scatter(grads[2].astype(jnp.bfloat16), 'narrow', scatter_dimensi...  142 us
    all_gather x1, waiting for transfers between devices, on_device(): lax.all_gather(w_down, 'narrow', axis=0, tiled=True)  95.4 us
    all_gather x1, waiting for transfers between devices, on_device(): lax.all_gather(w_up, 'narrow', axis=0, tiled=True)  94.2 us
    psum x1, blocking collectives, on_device(): lax.psum(totals[1].astype(jnp.bfloat16), 'wide').astype(jnp.float32)  64.3 us
    all_gather x1, waiting for transfers between devices, on_device(): lax.all_gather(w_qkv, 'narrow', axis=0, tiled=True)  62.6 us
  transfers between devices with their start and end apart: 19, of which 15 were waited for; matrix products, arithmetic and copies ran while one was open for 10% of the time, Pallas kernels for 0%

profile of v1, /device:TPU:0, one launch (start us, length us, event | category | flops | bytes accessed | tf_op | source)
XLA Modules:
  0.0 1364.3 jit_solution(12463062883724009330)
XLA Ops:
  10.1 5.3 all_gather.23
  15.4 4.4 all_gather.26
  19.8 4.4 all_gather.21
  24.2 4.6 all_gather.20
  30.1 62.6 %all-gather.7.cloned.1.call-done = bf16[1024,3072]{1,0:T(8,128)(2,1)} async-done(((bf16[512,3072]{1,0:T(8,128)(2,1)}), bf16[1024,3072]{1,0:T(8,128)(2,1)}) %all-gather.7.cloned.1.call-update) | async-done | bytes 6291472 | tf_op jit(solution)/shard_map/all_gather | solution.py:199
  92.7 3.9 fusion.2
  97.0 4.2 fusion.3
  104.4 23.1 %all-gather.9.cloned.1.call-done = bf16[1024,1024]{1,0:T(8,128)(2,1)} async-done(((bf16[512,1024]{1,0:T(8,128)(2,1)}), bf16[1024,1024]{1,0:T(8,128)(2,1)}) %all-gather.9.cloned.1.call-update) | async-done | bytes 2097168 | tf_op jit(solution)/shard_map/all_gather | solution.py:200
  138.8 94.2 %all-gather.11.cloned.1.call-done = bf16[1024,4096]{1,0:T(8,128)(2,1)} async-done(((bf16[512,4096]{1,0:T(8,128)(2,1)}), bf16[1024,4096]{1,0:T(8,128)(2,1)}) %all-gather.11.cloned.1.call-update) | async-done | bytes 8388624 | tf_op jit(solution)/shard_map/all_gather | solution.py:201
  233.0 10.0 multiply_convert_fusion
  243.0 95.4 %all-gather.13.cloned.1.call-done = bf16[4096,1024]{1,0:T(8,128)(2,1)} async-done(((bf16[2048,1024]{1,0:T(8,128)(2,1)}), bf16[4096,1024]{1,0:T(8,128)(2,1)}) %all-gather.13.cloned.1.call-update) | async-done | bytes 8388624 | tf_op jit(solution)/shard_map/all_gather | solution.py:202
  338.4 5.2 fusion.154
  344.5 9.2 multiply_convert_fusion.1
  360.9 5.7 fusion.127
  366.6 2.9 fusion.156
  369.5 5.7 fusion.126
  376.2 3.6 multiply_reduce_fusion.4
  388.2 3.0 convolution_convert_fusion.7
  395.6 2.9 convolution_bitcast_fusion
  402.9 4.7 convolution_convert_fusion.4
  414.5 4.6 convolution_convert_fusion.5
  420.2 7.1 convolution_convert_fusion.2
  427.4 7.2 convolution_convert_fusion.3
  435.8 5.6 convolution_convert_fusion
  442.7 5.6 convolution_convert_fusion.1
  450.8 5.1 fusion.157
  455.9 5.1 fusion.53
  468.1 2.9 add_convert_fusion.3
  471.0 62.1 %reduce-scatter.29.cloned.1.call-done = bf16[512,3072]{1,0:T(8,128)(2,1)} async-done(((bf16[1024,3072]{1,0:T(8,128)(2,1)}), bf16[512,3072]{1,0:T(8,128)(2,1)}) %reduce-scatter.29.cloned.1.call-update) | async-done | bytes 3145744 | tf_op jit(solution)/shard_map/reduce_scatter | solution.py:228
  533.1 79.5 %reduce-scatter.27.cloned.1.call-done = bf16[512,3072]{1,0:T(8,128)(2,1)} async-done(((bf16[1024,3072]{1,0:T(8,128)(2,1)}), bf16[512,3072]{1,0:T(8,128)(2,1)}) %reduce-scatter.27.cloned.1.call-update) | async-done | bytes 3145744 | tf_op jit(solution)/shard_map/reduce_scatter | solution.py:228
  612.6 5.7 add_convert_fusion.2
  618.3 96.6 %reduce-scatter.37.cloned.1.call-done = bf16[512,4096]{1,0:T(8,128)(2,1)} async-done(((bf16[1024,4096]{1,0:T(8,128)(2,1)}), bf16[512,4096]{1,0:T(8,128)(2,1)}) %reduce-scatter.37.cloned.1.call-update) | async-done | bytes 4194320 | tf_op jit(solution)/shard_map/reduce_scatter | solution.py:234
  714.9 102.1 %reduce-scatter.35.cloned.1.call-done = bf16[512,4096]{1,0:T(8,128)(2,1)} async-done(((bf16[1024,4096]{1,0:T(8,128)(2,1)}), bf16[512,4096]{1,0:T(8,128)(2,1)}) %reduce-scatter.35.cloned.1.call-update) | async-done | bytes 4194320 | tf_op jit(solution)/shard_map/reduce_scatter | solution.py:234
  816.9 7.2 add_convert_fusion.1
  824.2 94.4 %reduce-scatter.41.cloned.1.call-done = bf16[2048,1024]{1,0:T(8,128)(2,1)} async-done(((bf16[4096,1024]{1,0:T(8,128)(2,1)}), bf16[2048,1024]{1,0:T(8,128)(2,1)}) %reduce-scatter.41.cloned.1.call-update) | async-done | bytes 4194320 | tf_op jit(solution)/shard_map/reduce_scatter | solution.py:237
  918.6 101.5 %reduce-scatter.39.cloned.1.call-done = bf16[2048,1024]{1,0:T(8,128)(2,1)} async-done(((bf16[4096,1024]{1,0:T(8,128)(2,1)}), bf16[2048,1024]{1,0:T(8,128)(2,1)}) %reduce-scatter.39.cloned.1.call-update) | async-done | bytes 4194320 | tf_op jit(solution)/shard_map/reduce_scatter | solution.py:237
  1020.1 7.6 add_convert_fusion
  1029.6 6.9 all-reduce.4
  1039.7 8.4 reduce-scatter.43.cloned.1.call-done
  1049.0 21.5 %all-gather.1 = bf16[16,4,512]{2,1,0:T(4,128)(2,1)S(1)} all-gather(bf16[1,4,512]{2,1,0:T(4,128)(2,1)S(1)} %fusion.102), channel_id=2, replica_groups=mesh['wide'=16,'narrow'=2] {'wide'}, dimensions={0}, use_global_device_ids=true | all-gather | bytes 69632 | tf_op jit(solution)/shard_map/all_gather | solution.py:251
  1072.2 3.6 reduce-scatter.47.cloned.1.call-done
  1076.8 12.9 reduce-scatter.53.cloned.1.call-done
  1090.7 12.9 reduce-scatter.51.cloned.1.call-done
  1104.6 64.3 %all-reduce.2 = (bf16[4,512]{1,0:T(4,128)(2,1)S(1)}, bf16[4,512]{1,0:T(4,128)(2,1)S(1)}, bf16[2048]{0:T(1024)(128)(2,1)S(1)}) all-reduce(bf16[4,512]{1,0:T(4,128)(2,1)S(1)} %add_convert_fusion.18, bf16[4,512]{1,0:T(4,128)(2,1)S(1)} %add_convert_fusion.17, ...), channel_id=1, replica_groups=mesh['wide'=16,'narrow'=2] {'wide'}, use_global_device_ids=true, to_apply=%region_60.61 | all-reduce | flops 6144 | bytes 24576 | tf_op jit(solution)/shard_map/psum | solution.py:254
  1170.6 170.9 %all-reduce.7.cloned.1.call-done = (bf16[512,3072]{1,0:T(8,128)(2,1)}, bf16[512,1024]{1,0:T(8,128)(2,1)}, bf16[512,4096]{1,0:T(8,128)(2,1)}, bf16[2048,1024]{1,0:T(8,128)(2,1)}) async-done(((bf16[512,3072]{1,0:T(8,128)(2,1)}, bf16[512,1024]{1,0:T(8,128)(2,1)}, bf16[512,4096]{1,0:T(8,128)(2,1)}, bf16[2048,1024]{1,0:T(8,128)(2,1)}), (bf16[512,3072]{1,0:T(8,128)(2,1)}, bf16[512,1024]{1,0:T(8,128)(2,1)}, ...) | async-done | bytes 12582928 | tf_op jit(solution)/shard_map/psum | solution.py:255
  1341.6 5.5 convert_element_type.456
  1348.7 4.5 convert_element_type.468
  1353.2 4.4 convert_element_type.474
  (321 shorter events, 77.8 us)
Async XLA Ops:
  7.2 85.5 %all-gather.7.cloned.1.call-start = ((), (), s32[]{:S(2)}) async-start(), calls=%async_computation.14 | async-start | bytes 9437184 | tf_op jit(solution)/shard_map/all_gather | solution.py:199
  7.9 119.5 %all-gather.9.cloned.1.call-start = ((), (), s32[]{:S(2)}) async-start(), calls=%async_computation.15 | async-start | bytes 3145728 | tf_op jit(solution)/shard_map/all_gather | solution.py:200
  8.7 224.3 %all-gather.11.cloned.1.call-start = ((), (), s32[]{:S(2)}) async-start(), calls=%async_computation.16 | async-start | bytes 12582912 | tf_op jit(solution)/shard_map/all_gather | solution.py:201
  9.4 6.0 copy-start.47
  9.4 10.4 copy-start.48
  9.4 14.7 %copy-start.49 = (bf16[4,512]{1,0:T(4,128)(2,1)S(1)}, bf16[4,512]{1,0:T(4,128)(2,1)}, u32[]{:S(2)}) copy-start(bf16[4,512]{1,0:T(4,128)(2,1)} %param.16) | copy-start | bytes 12292
  9.4 19.3 %copy-start.2 = (bf16[2,1,128,1024]{3,2,1,0:T(8,128)(2,1)S(1)}, bf16[2,1,128,1024]{3,2,1,0:T(8,128)(2,1)}, u32[]{:S(2)}) copy-start(bf16[2,1,128,1024]{3,2,1,0:T(8,128)(2,1)} %param.12) | copy-start | bytes 1572868
  9.4 19.4 %copy-start.60 = (s32[16]{0:T(128)S(1)}, s32[16]{0:T(128)}, u32[]{:S(2)}) copy-start(s32[16]{0:T(128)} %param.15) | copy-start | bytes 196
  9.5 19.4 %copy-start.61 = (s32[2,1]{0,1:T(1,128)S(1)}, s32[2,1]{0,1:T(1,128)}, u32[]{:S(2)}) copy-start(s32[2,1]{0,1:T(1,128)} %param.14) | copy-start | bytes 28
  9.5 328.9 %all-gather.13.cloned.1.call-start = ((), (), s32[]{:S(2)}) async-start(), calls=%async_computation.17 | async-start | bytes 12582912 | tf_op jit(solution)/shard_map/all_gather | solution.py:202
  10.0 458.0 %reduce-scatter.33.cloned.1.call-start = ((), (), s32[]{:S(2)}) async-start(), calls=%async_computation.21 | async-start | bytes 3145728 | tf_op jit(solution)/shard_map/reduce_scatter | solution.py:231
  29.4 67.2 %copy-start.52 = (f32[128]{0:T(128)}, f32[128]{0:T(128)S(1)}, u32[]{:S(2)}) copy-start(f32[128]{0:T(128)S(1)} %get-tuple-element.41) | copy-start | bytes 1540
  96.9 6.4 copy-start.18
  101.5 30.6 %copy-start.20 = (bf16[128,3072]{0,1:T(8,128)(2,1)}, bf16[128,3072]{0,1:T(8,128)(2,1)S(1)}, u32[]{:S(2)}) copy-start(bf16[128,3072]{0,1:T(8,128)(2,1)S(1)} %copy.66) | copy-start | bytes 2359300
  104.4 27.7 %copy-start.34 = (bf16[16,64,128]{2,1,0:T(8,128)(2,1)}, bf16[16,64,128]{2,1,0:T(8,128)(2,1)S(1)}, u32[]{:S(2)}) copy-start(bf16[16,64,128]{2,1,0:T(8,128)(2,1)S(1)} %convolution_convert_fusion.11) | copy-start | bytes 786436
  130.6 6.5 copy-start.54
  137.0 106.0 %copy-start.56 = (f32[128]{0:T(128)}, f32[128]{0:T(128)S(1)}, u32[]{:S(2)}) copy-start(f32[128]{0:T(128)S(1)} %multiply_reduce_fusion.14) | copy-start | bytes 1540
  138.8 104.3 %copy-start.58 = (f32[128]{0:T(128)}, f32[128]{0:T(128)S(1)}, u32[]{:S(2)}) copy-start(f32[128]{0:T(128)S(1)} %multiply_reduce_fusion.16) | copy-start | bytes 1540
  338.4 6.1 copy-start.1
  338.4 16.3 %slice-start = ((s8[8388608]{0:T(1024)(128)(4,1)}), s8[4194304]{0:T(1024)(128)(4,1)S(1)}, s32[]{:S(2)}) async-start(s8[8388608]{0:T(1024)(128)(4,1)} %bitcast.288), calls=%async_computation.33 | async-start | bytes 8388608
  344.5 10.2 slice-start.1
  360.7 5.9 copy-start.40
  360.9 8.7 copy-start.38
  376.2 3.8 copy-start.59
  387.0 81.1 %reduce-scatter.31.cloned.1.call-start = ((), (), s32[]{:S(2)}) async-start(), calls=%async_computation.20 | async-start | bytes 3145728 | tf_op jit(solution)/shard_map/reduce_scatter | solution.py:231
  391.3 141.9 %reduce-scatter.29.cloned.1.call-start = ((), (), s32[]{:S(2)}) async-start(), calls=%async_computation.19 | async-start | bytes 9437184 | tf_op jit(solution)/shard_map/reduce_scatter | solution.py:228
  407.6 205.0 %reduce-scatter.27.cloned.1.call-start = ((), (), s32[]{:S(2)}) async-start(), calls=%async_computation.18 | async-start | bytes 9437184 | tf_op jit(solution)/shard_map/reduce_scatter | solution.py:228
  419.2 295.7 %reduce-scatter.37.cloned.1.call-start = ((), (), s32[]{:S(2)}) async-start(), calls=%async_computation.23 | async-start | bytes 12582912 | tf_op jit(solution)/shard_map/reduce_scatter | solution.py:234
  427.3 389.6 %reduce-scatter.35.cloned.1.call-start = ((), (), s32[]{:S(2)}) async-start(), calls=%async_computation.22 | async-start | bytes 12582912 | tf_op jit(solution)/shard_map/reduce_scatter | solution.py:234
  434.6 484.0 %reduce-scatter.41.cloned.1.call-start = ((), (), s32[]{:S(2)}) async-start(), calls=%async_computation.25 | async-start | bytes 12582912 | tf_op jit(solution)/shard_map/reduce_scatter | solution.py:237
  441.5 578.7 %reduce-scatter.39.cloned.1.call-start = ((), (), s32[]{:S(2)}) async-start(), calls=%async_computation.24 | async-start | bytes 12582912 | tf_op jit(solution)/shard_map/reduce_scatter | solution.py:237
  448.4 590.3 %reduce-scatter.45.cloned.1.call-start = ((), (), s32[]{:S(2)}) async-start(), calls=%async_computation.27 | async-start | bytes 393216
  455.8 5.1 copy-start.53
  455.9 5.2 copy-start.51
  455.9 6.7 copy-start.45
  462.6 585.4 %reduce-scatter.43.cloned.1.call-start = ((), (), s32[]{:S(2)}) async-start(), calls=%async_computation.26 | async-start | bytes 393216
  463.7 607.5 %reduce-scatter.49.cloned.1.call-start = ((), (), s32[]{:S(2)}) async-start(), calls=%async_computation.29 | async-start | bytes 393216
  464.7 611.1 %reduce-scatter.47.cloned.1.call-start = ((), (), s32[]{:S(2)}) async-start(), calls=%async_computation.28 | async-start | bytes 393216
  465.9 623.8 %reduce-scatter.53.cloned.1.call-start = ((), (), s32[]{:S(2)}) async-start(), calls=%async_computation.31 | async-start | bytes 393216
  467.0 636.5 %reduce-scatter.51.cloned.1.call-start = ((), (), s32[]{:S(2)}) async-start(), calls=%async_computation.30 | async-start | bytes 393216
  468.0 873.6 %all-reduce.7.cloned.1.call-start = ((), (), s32[]{:S(2)}) async-start(), calls=%async_computation.32 | async-start | bytes 25165824 | tf_op jit(solution)/shard_map/psum | solution.py:255
  1027.7 8.8 copy-start.36
  1027.7 8.8 copy-start.37
  1027.7 9.7 copy-start.23
  1027.7 9.7 copy-start.25
  1341.6 5.5 copy-start.33
  1341.6 7.1 copy-start.27
  1348.7 4.5 copy-start.26
  (36 other events, 58.3 us)
Sparse Core Ops, SparseCore 0:
  9.5 83.1 all-gather.6
  94.2 33.1 all-gather.8
  129.0 103.9 all-gather.10
  234.4 103.9 all-gather.12
  387.1 31.8 reduce-scatter.32
  421.2 31.8 reduce-scatter.30
  456.0 77.1 reduce-scatter.28
  535.4 77.1 reduce-scatter.26
  615.5 99.3 reduce-scatter.36
  717.6 99.3 reduce-scatter.34
  819.2 99.3 reduce-scatter.40
  920.7 99.3 reduce-scatter.38
  1022.3 11.7 reduce-scatter.44
  1036.2 11.7 reduce-scatter.42
  1050.1 11.7 reduce-scatter.48
  1064.0 11.7 reduce-scatter.46
  1077.9 11.7 reduce-scatter.52
  1091.7 11.7 reduce-scatter.50
  1108.7 232.8 all-reduce.6
